TPU v7x, 768 devices: a whole 4x8x12 slice. The times are simulated.
768 devices in a mesh: expert: 96 (over z, y), etp: 8 (over x, core).
Axes of the slice: x: 4, y: 8, z: 12, core: 2. Of those that a mesh axis runs over, the one named last changes fastest.
Arguments:
- hidden_in: bfloat16 [1152, 4096], P('expert', 'etp'), may hold values from -6 to 6
- expert_ids: int32 [1152, 8], P('expert'), may hold values from 0 to 95, all different within a row; in each aligned block of 12 rows (0 to 11, 12 to 23, ...) at most 2 rows name the same one
- gate_weights: float32 [1152, 8], P('expert'), may hold values from 0.2 to 1
- out_grad: bfloat16 [1152, 4096], P('expert', 'etp'), may hold values from -6 to 6
- gate_weight: bfloat16 [96, 4096, 1024], P('expert', None, 'etp'), may hold values from -0.09375 to 0.09375
- up_weight: bfloat16 [96, 4096, 1024], P('expert', None, 'etp'), may hold values from -0.09375 to 0.09375
- down_weight: bfloat16 [96, 1024, 4096], P('expert', 'etp'), may hold values from -0.1875 to 0.1875
Outputs:
- mixed_out: bfloat16 [1152, 4096], P('expert', 'etp')
- input_grad: bfloat16 [1152, 4096], P('expert', 'etp')
- down_grad: bfloat16 [96, 1024, 4096], P('expert', 'etp')
Inputs may be any that keep to these rules, and one draw needn't show every extreme that they name: `expert_ids`: each token names 8 different experts. Within each aligned block of 12 tokens no expert is named by more than 2 tokens, and in some block an expert is named by exactly 2 tokens.
All inputs are finite; a program needn't handle non-finite values.
Results may differ from a plain program's by a relative error of at most 0.018.
Values may be sent and summed in bfloat16 or wider, within the bound.
A program may use at most 32 MiB of HBM per device.

v0:
```python
import jax
import jax.numpy as jnp
from jax import lax
from jax.sharding import PartitionSpec as P


def sent_together(arrays, axis, split_dim, concat_dim, along):
    ends, at = ([], 0)
    for a in arrays[:-1]:
        at += a.shape[along]
        ends.append(at)
    both = jnp.concatenate(arrays, axis=along)
    return tuple(
        jnp.split(
            lax.all_to_all(both, axis, split_axis=split_dim, concat_axis=concat_dim, tiled=True),
            ends,
            axis=along,
        )
    )


def side_by_side(arrays, axis, dim, along):
    widths = [a.shape[along] for a in arrays]
    both = jnp.concatenate(arrays, axis=along)
    whole = lax.all_gather(both, axis, axis=dim, tiled=True)
    return tuple(jnp.split(whole, [sum(widths[:k]) for k in range(1, len(widths))], axis=along))


def split_up(shard, dim, length):
    shape = shard.shape
    pieces = shard.reshape(*shape[:dim], length, shape[dim] // length, *shape[dim + 1 :])
    return jnp.moveaxis(pieces, dim, 0)


def summed_on_arrival(shard, axis, dim):
    pieces = split_up(shard, dim, lax.axis_size(axis))
    arrived = lax.all_to_all(pieces, axis, split_axis=0, concat_axis=0, tiled=True)
    return arrived.astype(jnp.float32).sum(axis=0)


def sent_together_2(arrays, axis, dim, along):
    widths = [a.shape[along] for a in arrays]
    both = jnp.concatenate(arrays, axis=along)
    whole = summed_on_arrival(both, axis, dim)
    return tuple(jnp.split(whole, [sum(widths[:k]) for k in range(1, len(widths))], axis=along))


def route_tables(expert_ids, experts, capacity):
    token_count, per_token = expert_ids.shape
    flat_ids = expert_ids.reshape(-1)
    onehot = (flat_ids[:, None] == jnp.arange(experts, dtype=jnp.int32)[None, :]).astype(jnp.int32)
    slot_rank = jnp.sum((jnp.cumsum(onehot, axis=0) - onehot) * onehot, axis=1)
    position = flat_ids * capacity + slot_rank
    placing = (
        jnp.arange(experts * capacity, dtype=jnp.int32)[:, None] == position[None, :]
    ).astype(jnp.float32)
    token_place = jnp.sum(placing.reshape(experts * capacity, token_count, per_token), axis=2)
    return (position, placing.astype(jnp.bfloat16), token_place.astype(jnp.bfloat16))


def contract_last(left, right):
    return lax.dot_general(
        left, right, (((1,), (1,)), ((), ())), preferred_element_type=jnp.float32
    )


def on_device(hidden_in, expert_ids, gate_weights, out_grad, gate_weight, up_weight, down_weight):
    token_count, per_token = expert_ids.shape
    experts = lax.axis_size("expert")
    capacity = min(token_count, token_count * per_token // experts + 1)
    width = gate_weight.shape[1]
    slice_width = hidden_in.shape[1]
    position, placing, token_place = route_tables(expert_ids, experts, capacity)
    gate_flat = gate_weights.reshape(-1)
    feature_count = hidden_in.shape[1]
    grad_slots = (
        jnp.repeat(out_grad.astype(jnp.float32), per_token, axis=0) * gate_flat[:, None]
    ).astype(jnp.bfloat16)
    rows_part = jnp.dot(token_place, hidden_in, preferred_element_type=jnp.float32).astype(
        jnp.bfloat16
    )
    grad_rows = jnp.dot(placing, grad_slots, preferred_element_type=jnp.float32).astype(
        jnp.bfloat16
    )
    send_in = rows_part.reshape(experts, capacity, feature_count)
    send_grad = grad_rows.reshape(experts, capacity, feature_count)
    part_in, part_grad = sent_together((send_in, send_grad), "expert", 0, 0, 1)
    rows_in, grad_in = side_by_side((part_in, part_grad), "etp", 2, 0)
    rows_in = rows_in.reshape(experts * capacity, width)
    grad_in = grad_in.reshape(experts * capacity, width)
    gate_matrix = gate_weight[0]
    up_matrix = up_weight[0]
    down_matrix = down_weight[0]
    gate_pre = jnp.dot(rows_in, gate_matrix, preferred_element_type=jnp.float32)
    up_pre = jnp.dot(rows_in, up_matrix, preferred_element_type=jnp.float32)
    sigmoid_gate = jax.nn.sigmoid(gate_pre)
    swish_gate = gate_pre * sigmoid_gate
    hidden_act = (swish_gate * up_pre).astype(jnp.bfloat16)
    out_part = jnp.dot(hidden_act, down_matrix, preferred_element_type=jnp.float32)
    act_grad = contract_last(grad_in, down_matrix)
    down_grad = lax.dot_general(
        hidden_act, grad_in, (((0,), (0,)), ((), ())), preferred_element_type=jnp.float32
    ).astype(jnp.bfloat16)
    gate_grad = (act_grad * up_pre * sigmoid_gate * (1.0 + gate_pre * (1.0 - sigmoid_gate))).astype(
        jnp.bfloat16
    )
    up_grad = (act_grad * swish_gate).astype(jnp.bfloat16)
    input_part = contract_last(gate_grad, gate_matrix) + contract_last(up_grad, up_matrix)
    out_sum, input_sum = sent_together_2(
        (out_part.astype(jnp.bfloat16), input_part.astype(jnp.bfloat16)), "etp", 1, 0
    )
    expert_out = out_sum.astype(jnp.bfloat16).reshape(experts, capacity, slice_width)
    slot_grad = input_sum.astype(jnp.bfloat16).reshape(experts, capacity, slice_width)
    back_out, back_grad = sent_together((expert_out, slot_grad), "expert", 0, 0, 1)
    picked = jnp.take(back_out.reshape(experts * capacity, slice_width), position, axis=0)
    picked = picked.astype(jnp.float32).reshape(token_count, per_token, slice_width)
    mixed_out = jnp.sum(picked * gate_weights[:, :, None], axis=1).astype(jnp.bfloat16)
    returned = jnp.take(back_grad.reshape(experts * capacity, slice_width), position, axis=0)
    returned = returned.astype(jnp.float32).reshape(token_count, per_token, slice_width)
    input_grad = jnp.sum(returned, axis=1).astype(jnp.bfloat16)
    return (mixed_out, input_grad, down_grad[None])


def solution(mesh):
    return jax.shard_map(
        on_device,
        mesh=mesh,
        in_specs=(
            P("expert", "etp"),
            P("expert", None),
            P("expert", None),
            P("expert", "etp"),
            P("expert", None, "etp"),
            P("expert", None, "etp"),
            P("expert", "etp", None),
        ),
        out_specs=(P("expert", "etp"), P("expert", "etp"), P("expert", "etp", None)),
        check_vma=False,
    )
```

profile of v0, /device:TPU:1, one launch (start us, length us, event | category | flops | bytes accessed | tf_op | source)
XLA Modules:
  0.0 201.3 jit_solution(13265845207321957203)
XLA Ops:
  7.2 0.0 copy-start
  7.2 0.0 all-gather.2.cloned.1.call-start
  7.2 0.8 copy.23
  8.1 0.1 eq.36
  8.2 0.1 fusion.20
  8.3 0.1 reduce_window_sum.11
  8.4 0.2 select_reduce_fusion
  8.6 0.1 reduce_sum.48
  8.7 0.8 copy.25
  9.4 0.1 mul.62
  9.5 0.7 convert_element_type.64
  10.3 0.1 convert_reduce_fusion
  10.4 0.3 convolution_convert_fusion.3
  10.6 0.1 reshape.77
  10.7 1.0 convolution_convert_fusion.2
  11.7 0.1 reshape.75
  11.8 0.4 pad_maximum_fusion.1
  12.2 44.0 %all_to_all.15 = bf16[96,4,512]{2,1,0:T(4,128)(2,1)S(1)} all-to-all(bf16[96,4,512]{2,1,0:T(4,128)(2,1)S(1)} %pad_maximum_fusion.1), channel_id=1, replica_groups=mesh['expert'=96,'etp'=8] {'expert'}, dimensions={0} | all-to-all | bytes 786432 | tf_op jit(solution)/shard_map/all_to_all | solution.py:15
  56.2 0.3 fusion.28
  56.5 1.3 pad_maximum_fusion.2
  57.7 0.0 all-gather.2.cloned.1.call-update
  57.7 32.5 %all-gather.2.cloned.1.call-done = bf16[192,2,4096]{2,1,0:T(2,128)(2,1)} async-done(((bf16[192,2,512]{2,1,0:T(2,128)(2,1)}), bf16[192,2,4096]{2,1,0:T(2,128)(2,1)}) %all-gather.2.cloned.1.call-update) | async-done | bytes 3145744 | tf_op jit(solution)/shard_map/all_gather | solution.py:25
  90.2 5.7 %fusion.25 = (bf16[96,2,4096]{2,1,0:T(2,128)(2,1)}, bf16[96,2,4096]{2,1,0:T(2,128)(2,1)}) fusion(bf16[192,2,4096]{2,1,0:T(2,128)(2,1)} %all-gather.2.cloned.1.call-done), kind=kLoop, calls=%fused_computation.53 | loop fusion | bytes 6291456 | tf_op jit(solution)/shard_map/split | solution.py:26
  95.9 2.5 %reshape.79 = bf16[192,4096]{1,0:T(8,128)(2,1)S(1)} reshape(bf16[96,2,4096]{2,1,0:T(2,128)(2,1)} %get-tuple-element.6) | data formatting | bytes 3145728 | tf_op jit(solution)/shard_map/reshape | solution.py:90
  98.4 3.7 %reshape.78 = bf16[192,4096]{1,0:T(8,128)(2,1)} reshape(bf16[96,2,4096]{2,1,0:T(2,128)(2,1)} %get-tuple-element.7) | data formatting | bytes 3145728 | tf_op jit(solution)/shard_map/reshape | solution.py:89
  102.1 0.0 copy-start.1
  102.1 0.0 copy-start.2
  102.1 1.9 fusion.2
  104.1 0.0 copy-done.1
  104.1 0.1 copy-done.2
  104.1 0.6 fusion.10
  104.7 0.0 copy-done
  104.7 0.0 copy-start.3
  104.7 0.6 multiply_convert_fusion.2
  105.3 0.6 copy-done.3
  105.9 0.6 convolution_convert_fusion
  106.5 0.6 fusion.8
  107.1 0.6 fusion
  107.7 0.3 pad_maximum_fusion
  108.0 0.3 copy.30
  108.3 41.2 %all_to_all.16 = bf16[8,384,512]{2,1,0:T(8,128)(2,1)} all-to-all(bf16[8,384,512]{2,1,0:T(8,128)(2,1)S(1)} %bitcast.45), channel_id=1, replica_groups=mesh['expert'=96,'etp'=8] {'etp'}, dimensions={0} | all-to-all | bytes 6291456 | tf_op jit(solution)/shard_map/all_to_all | solution.py:37
  149.6 2.5 %reduce = bf16[384,512]{1,0:T(8,128)(2,1)S(1)} reduce(bf16[8,384,512]{2,1,0:T(8,128)(2,1)} %all_to_all.16, bf16[]{:T(256)} %constant.29), dimensions={0}, to_apply=%region_3.4.clone | reduce | flops 1376256 | bytes 3538946 | tf_op jit(solution)/shard_map/reduce_sum | solution.py:38
  152.1 0.1 reshape.81
  152.2 0.1 reshape.82
  152.3 1.1 pad_maximum_fusion.3
  153.4 16.4 %all-to-all-start.2 = ((bf16[96,4,512]{2,1,0:T(4,128)(2,1)}), bf16[96,4,512]{2,1,0:T(4,128)(2,1)S(1)}, u32[]{:S(2)}, u32[]{:S(2)}) async-start(bf16[96,4,512]{2,1,0:T(4,128)(2,1)} %pad_maximum_fusion.3), calls=%async_computation.2 | async-start | bytes 786432 | tf_op jit(solution)/shard_map/all_to_all | solution.py:15
  169.8 1.4 fusion.1
  171.3 19.7 %all-to-all-done.2 = bf16[96,4,512]{2,1,0:T(4,128)(2,1)S(1)} async-done(((bf16[96,4,512]{2,1,0:T(4,128)(2,1)}), bf16[96,4,512]{2,1,0:T(4,128)(2,1)S(1)}, u32[]{:S(2)}, u32[]{:S(2)}) %all-to-all-start.2) | async-done | bytes 393248 | tf_op jit(solution)/shard_map/all_to_all | solution.py:15
  191.0 0.3 fusion.26
  191.3 0.1 reshape.86
  191.4 0.1 reshape.83
  191.4 0.8 gather_fusion.1
  192.2 0.8 gather_fusion
  193.0 0.7 bitcast_reduce_fusion
  193.7 0.8 fusion.12
  (5 shorter events, 0.1 us)
Async XLA Ops:
  7.2 97.5 %copy-start = (bf16[1,4096,128]{2,1,0:T(8,128)(2,1)S(1)}, bf16[1,4096,128]{2,1,0:T(8,128)(2,1)}, u32[]{:S(2)}) copy-start(bf16[1,4096,128]{2,1,0:T(8,128)(2,1)} %param.14) | copy-start | bytes 3145732
  7.2 83.0 %all-gather.2.cloned.1.call-start = ((), (), s32[]{:S(2)}) async-start(), calls=%async_computation.3 | async-start | bytes 3538944 | tf_op jit(solution)/shard_map/all_gather | solution.py:25
  102.1 1.9 copy-start.1
  102.1 2.0 copy-start.2
  104.7 1.2 copy-start.3
  153.4 37.6 %all-to-all-start.2 = ((bf16[96,4,512]{2,1,0:T(4,128)(2,1)}), bf16[96,4,512]{2,1,0:T(4,128)(2,1)S(1)}, u32[]{:S(2)}, u32[]{:S(2)}) async-start(bf16[96,4,512]{2,1,0:T(4,128)(2,1)} %pad_maximum_fusion.3), calls=%async_computation.2 | async-start | bytes 786432 | tf_op jit(solution)/shard_map/all_to_all | solution.py:15
Sparse Core Ops, SparseCore 0:
  57.9 32.3 all-gather.1
where the time goes:
time: 204 us; the launch traced here: 201 us
  blocking collectives  85.2 us (42%)
  waiting for transfers between devices  52.2 us (26%)
  local copies, waits for them, and re-layouts  17.4 us (9%)
  starting transfers between devices  16.4 us (8%)
  between operations  14.3 us (7%)
  other arithmetic  8.4 us (4%)
  matrix products  7.45 us (4%)
    all_to_all x1, blocking collectives, sent_together(): lax.all_to_all(both, axis, split_axis=split_dim, concat_axis=concat_dim,...  44 us
    all_to_all x1, blocking collectives, summed_on_arrival(): lax.all_to_all(pieces, axis, split_axis=0, concat_axis=0, tiled=True)  41.2 us
    all_gather x1, waiting for transfers between devices, side_by_side(): whole = lax.all_gather(both, axis, axis=dim, tiled=True)  32.5 us
    all_to_all x1, waiting for transfers between devices, sent_together(): lax.all_to_all(both, axis, split_axis=split_dim, concat_axis=concat_dim,...  19.7 us
    all_to_all x1, starting transfers between devices, sent_together(): lax.all_to_all(both, axis, split_axis=split_dim, concat_axis=concat_dim,...  16.4 us
    split x1, local copies, waits for them, and re-layouts, side_by_side(): jnp.split(whole, [sum(widths[:k]) for k in range(1, len(widths))], axis=a...  5.73 us
  transfers between devices with their start and end apart: 2, of which 2 were waited for; matrix products, arithmetic and copies ran while one was open for 1% of the time, Pallas kernels for 0%

commit v1 on v0

v1 whole, which is shorter than its diff:
```python
import functools

import jax
import jax.numpy as jnp
from jax import lax
from jax.experimental import pallas as pl
from jax.experimental.pallas import tpu as pltpu
from jax.sharding import PartitionSpec as P

MESH = pl.DeviceIdType.MESH
CAP = 2
PAD = 16
NX, NC = 4, 2
NY = 8
F32, BF16 = jnp.float32, jnp.bfloat16


def ring_offsets(n):
    out = [0]
    for k in range(1, n // 2 + 1):
        out.append(k)
        if k != n - k:
            out.append(n - k)
    return out


def nn(a, b):
    return lax.dot_general(a, b, (((1,), (0,)), ((), ())), preferred_element_type=F32)


def nt(a, b):
    return lax.dot_general(a, b, (((1,), (1,)), ((), ())), preferred_element_type=F32)


def tn(a, b, precision=None):
    return lax.dot_general(
        a, b, (((0,), (0,)), ((), ())), precision=precision, preferred_element_type=F32
    )


class Sems:
    def __init__(self):
        self.index = {}

    def at(self, key):
        return self.index.setdefault(key, len(self.index))


def kernel(nz, chunks, sizes, *refs):
    (hid, ids, gat, og, wg_hbm, wu_hbm, wd_hbm) = refs[:7]
    (mix_o, ing_o, dgr_o) = refs[7:10]
    (tok, rt, zs, g, wgu, dn, asc, csc, gsc, sel, selg, pre, agr, hact, gug, dgr) = refs[10:26]
    (pps, ppr, chip, d2r, nbr, fin, ret, ys, yr, send_sem, recv_sem, loc_sem) = refs[26:]
    token_count, width, hidden = sizes
    x_t = lax.axis_index("etp")
    x_e = lax.axis_index("expert")
    x, c = x_t // NC, x_t % NC
    z, y = x_e // NY, x_e % NY
    offs = ring_offsets(nz)
    group = NY * CAP
    rows = nz * group
    lanes = NY * PAD
    half = lanes // 2
    crow = rows // chunks
    per = nz // chunks
    slots = NX * NC

    def neg(p):
        return offs.index((nz - offs[p]) % nz)

    def zdev(p):
        return (lax.rem(z + offs[p], nz) * NY + y, x_t)

    def ydev(d):
        return (z * NY + lax.rem(y + d, NY), x_t)

    def tab(dx, other=0):
        return lax.rem(x + dx, NX) * NC + (1 - c if other else c)

    def xdev(dx):
        return (x_e, tab(dx))

    partner = (x_e, tab(0, 1))
    ssems, rsems, sends = Sems(), Sems(), []

    def put(src, dst, key_here, key_there, dev):
        copy = pltpu.make_async_remote_copy(
            src_ref=src,
            dst_ref=dst,
            send_sem=send_sem.at[ssems.at(key_here)],
            recv_sem=recv_sem.at[rsems.at(key_there)],
            device_id=dev,
            device_id_type=MESH,
        )
        copy.start()
        sends.append(copy)

    def got(dst, key, dev):
        pltpu.make_async_remote_copy(
            src_ref=dst,
            dst_ref=dst,
            send_sem=send_sem.at[0],
            recv_sem=recv_sem.at[rsems.at(key)],
            device_id=dev,
            device_id_type=MESH,
        ).wait_recv()

    loads = []
    for t in range(slots):
        cols = pl.ds(t * width, width)
        for src, dst in (
            (wg_hbm.at[cols, :], wgu.at[t, :, pl.ds(0, hidden)]),
            (wu_hbm.at[cols, :], wgu.at[t, :, pl.ds(hidden, hidden)]),
            (wd_hbm.at[:, cols], dn.at[t]),
        ):
            copy = pltpu.make_async_copy(src, dst, loc_sem.at[len(loads)])
            copy.start()
            loads.append(copy)

    peers = [zdev(p) for p in range(1, nz)] + [ydev(d) for d in range(1, NY)]
    peers += [xdev(1), xdev(3), partner]
    barrier = pltpu.get_barrier_semaphore()
    for dev in peers:
        pl.semaphore_signal(barrier, inc=1, device_id=dev, device_id_type=MESH)

    for k, src in ((0, hid), (1, og)):
        tok[k, 0:PAD, :] = jnp.zeros((PAD, width), BF16)
        tok[k, 0:token_count, :] = src[...]
    lane_t = lax.broadcasted_iota(jnp.int32, (token_count, lanes), 1)
    row_t = lax.broadcasted_iota(jnp.int32, (token_count, lanes), 0)
    here = lax.rem(lane_t, PAD) == row_t
    exact = lax.Precision.HIGHEST
    rt[0] = tn(ids[...].astype(F32), jnp.where(here & (lane_t < half), 1.0, 0.0), exact) + tn(
        gat[...], jnp.where(here & (lane_t >= half), 1.0, 0.0), exact
    )

    pl.semaphore_wait(barrier, len(peers))

    y_order = sorted(range(1, NY), key=lambda d: -min(d, NY - d))
    for d in y_order:
        put(rt.at[0], rt.at[NY - d], ("rt", d), ("rt", NY - d), ydev(d))
    for k in (0, 1):
        for d in y_order:
            put(
                tok.at[k, pl.ds(0, PAD)],
                tok.at[k, pl.ds((NY - d) * PAD, PAD)],
                ("tok", k, d),
                ("tok", k, NY - d),
                ydev(d),
            )

    for d in range(1, NY):
        got(rt.at[d], ("rt", d), ydev(d))
    lane8 = lax.broadcasted_iota(jnp.int32, rt.shape[1:], 1)
    ids_all = jnp.full(rt.shape[1:], -1.0, F32)
    gates_all = jnp.zeros(rt.shape[1:], F32)
    for d in range(NY):
        straight = rt[d]
        turned = pltpu.roll(straight, half, 1)
        mine = (lane8 // PAD == d) & (lax.rem(lane8, PAD) < token_count)
        low = d < NY // 2
        ids_all = jnp.where(mine, straight if low else turned, ids_all)
        gates_all = jnp.where(mine, turned if low else straight, gates_all)
    ids_all = ids_all.astype(jnp.int32)
    asc[...] = jnp.zeros(asc.shape, F32)
    for p in range(nz):
        hit = ids_all == lax.rem(z + offs[p], nz) * NY + y
        asc[p : p + 1, :] = jnp.sum(jnp.where(hit, 1.0, 0.0), axis=0, keepdims=True)
        gsc[p : p + 1, :] = jnp.sum(jnp.where(hit, gates_all, 0.0), axis=0, keepdims=True)
    l0 = lax.broadcasted_iota(jnp.int32, (lanes, lanes), 0)
    l1 = lax.broadcasted_iota(jnp.int32, (lanes, lanes), 1)
    earlier = jnp.where((l0 // PAD == l1 // PAD) & (l0 < l1), 1.0, 0.0).astype(BF16)
    csc[...] = nn(asc[...].astype(BF16), earlier)
    r2 = lax.broadcasted_iota(jnp.int32, (group, lanes), 0)
    b2 = lax.broadcasted_iota(jnp.int32, (group, lanes), 1) // PAD
    block = jnp.where(r2 // CAP == b2, 1.0, 0.0)
    rank = lax.rem(r2, CAP).astype(F32)
    for p in range(nz):
        pick = jnp.where(csc[p : p + 1, :] == rank, block, 0.0) * asc[p : p + 1, :]
        sel[p * group : (p + 1) * group, :] = pick.astype(BF16)
        selg[p * group : (p + 1) * group, :] = pick * gsc[p : p + 1, :]

    z_order = sorted(range(1, nz), key=lambda p: -p)
    for k in (0, 1):
        for d in range(1, NY):
            got(tok.at[k, pl.ds(d * PAD, PAD)], ("tok", k, d), ydev(d))
        picked = nn(sel[...], tok[k])
        if k == 1:
            picked = picked * jnp.sum(selg[...], axis=1, keepdims=True)
        zs[k] = picked.astype(BF16)
        for p in z_order:
            q = neg(p)
            put(
                zs.at[k, pl.ds(p * group, group)],
                g.at[k, x_t, pl.ds(q * group, group)],
                ("z", k, p),
                ("z", k, q),
                zdev(p),
            )
        g[k, x_t, 0:group, :] = zs[k, 0:group, :]

    for copy in loads:
        copy.wait()

    def piece(k, j, t):
        return g.at[k, t, pl.ds(j * crow, crow)]

    def pass_own(k, j):
        for p in range(j * per, (j + 1) * per):
            if p:
                got(g.at[k, x_t, pl.ds(p * group, group)], ("z", k, p), zdev(p))
        own = piece(k, j, x_t)
        put(own, own, ("g", k, j, "own+"), ("g", k, j, 3), xdev(1))
        put(own, own, ("g", k, j, "own-"), ("g", k, j, 1), xdev(3))
        put(own, own, ("g", k, j, "own|"), ("g", k, j, "o0"), partner)

    def pass_near(k, j):
        for dx in (3, 1):
            ref = piece(k, j, tab(dx))
            got(ref, ("g", k, j, dx), xdev(dx))
            if (j % 2 == 0) == (dx == 3):
                put(ref, ref, ("g", k, j, "far"), ("g", k, j, 2), xdev(4 - dx))
            put(ref, ref, ("g", k, j, "near|", dx), ("g", k, j, "o%d" % dx), partner)

    def pass_far(k, j):
        ref = piece(k, j, tab(2))
        got(ref, ("g", k, j, 2), xdev(3))
        put(ref, ref, ("g", k, j, "far|"), ("g", k, j, "o2"), partner)

    steps = [(k, j) for k in (0, 1) for j in range(chunks)]

    def step(s):
        if 0 <= s < len(steps):
            pass_own(*steps[s])
        if 0 <= s - 1 < len(steps):
            pass_near(*steps[s - 1])
        if 0 <= s - 2 < len(steps):
            pass_far(*steps[s - 2])

    def wait_other(k):
        for dx in (0, 3, 1, 2):
            for j in range(chunks):
                got(piece(k, j, tab(dx, 1)), ("g", k, j, "o%d" % dx), partner)

    for s in range(chunks + 2):
        step(s)
    pre[...] = nn(g[0, tab(0)], wgu[tab(0)])
    for dx in (3, 1, 2):
        pre[...] += nn(g[0, tab(dx)], wgu[tab(dx)])
    wait_other(0)
    for dx in (0, 3, 1, 2):
        pre[...] += nn(g[0, tab(dx, 1)], wgu[tab(dx, 1)])
    gate_pre, up_pre = pre[:, 0:hidden], pre[:, hidden : 2 * hidden]
    hact[...] = (gate_pre * jax.nn.sigmoid(gate_pre) * up_pre).astype(BF16)

    def part(k, t):
        return nn(hact[...], dn[t]) if k == 0 else nt(gug[...], wgu[t])

    order = (2, 1, 3, 0)

    def reduce_pair_send(k):
        for dx in order:
            pps[k, dx] = part(k, tab(dx, 1)).astype(BF16)
            put(pps.at[k, dx], ppr.at[k, dx], ("pp", k, dx), ("pp", k, dx), partner)

    first, second = pl.ds(0, rows // 2), pl.ds(rows // 2, rows // 2)

    def reduce_pair(k, dx):
        mine = part(k, tab(dx))
        got(ppr.at[k, dx], ("pp", k, dx), partner)
        chip[k, dx] = (mine + ppr[k, dx].astype(F32)).astype(BF16)

    def reduce_start(k):
        reduce_pair(k, 2)
        put(chip.at[k, 2, first], d2r.at[k, 0], ("d2", k, 0), ("d2", k, 0), xdev(1))
        put(chip.at[k, 2, second], d2r.at[k, 1], ("d2", k, 1), ("d2", k, 1), xdev(3))
        reduce_pair(k, 1)
        put(chip.at[k, 1, second], nbr.at[k, 0, second], ("n", k, 0, 1), ("n", k, 0, 1), xdev(1))
        reduce_pair(k, 3)
        put(chip.at[k, 3, first], nbr.at[k, 1, first], ("n", k, 1, 0), ("n", k, 1, 0), xdev(3))
        reduce_pair(k, 0)

    def reduce_relay(k):
        for i, (dx, part_rows) in enumerate(((1, first), (3, second))):
            got(d2r.at[k, i], ("d2", k, i), xdev(4 - dx))
            chip[k, dx, part_rows] = (
                chip[k, dx, part_rows].astype(F32) + d2r[k, i].astype(F32)
            ).astype(BF16)
            put(
                chip.at[k, dx, part_rows],
                nbr.at[k, i, part_rows],
                ("n", k, i, i),
                ("n", k, i, i),
                xdev(dx),
            )

    def reduce_end(k):
        for i in (0, 1):
            for h, part_rows in enumerate((first, second)):
                got(nbr.at[k, i, part_rows], ("n", k, i, h), xdev(3 if i == 0 else 1))
        fin[k] = (
            chip[k, 0].astype(F32) + nbr[k, 0].astype(F32) + nbr[k, 1].astype(F32)
        ).astype(BF16)
        for p in z_order:
            q = neg(p)
            put(
                fin.at[k, pl.ds(p * group, group)],
                ret.at[k, pl.ds(q * group, group)],
                ("back", k, p),
                ("back", k, q),
                zdev(p),
            )
        ret[k, 0:group, :] = fin[k, 0:group, :]

    reduce_pair_send(0)
    step(chunks + 2)
    step(chunks + 3)
    reduce_start(0)
    for s in range(chunks + 4, 2 * chunks + 2):
        step(s)

    agr[...] = nt(g[1, tab(0)], dn[tab(0)])
    for dx in (3, 1, 2):
        agr[...] += nt(g[1, tab(dx)], dn[tab(dx)])
    wait_other(1)
    for dx in (0, 3, 1, 2):
        agr[...] += nt(g[1, tab(dx, 1)], dn[tab(dx, 1)])
    gate_pre, up_pre = pre[:, 0:hidden], pre[:, hidden : 2 * hidden]
    sig = jax.nn.sigmoid(gate_pre)
    act_grad = agr[...]
    gug[:, 0:hidden] = (act_grad * up_pre * sig * (1.0 + gate_pre * (1.0 - sig))).astype(BF16)
    gug[:, hidden : 2 * hidden] = (act_grad * (gate_pre * sig)).astype(BF16)

    reduce_pair_send(1)
    reduce_relay(0)
    reduce_start(1)
    reduce_end(0)
    reduce_relay(1)

    for t in range(slots):
        dgr[:, t * width : (t + 1) * width] = tn(hact[...], g[1, t]).astype(BF16)
    dgr_copy = pltpu.make_async_copy(dgr, dgr_o, loc_sem.at[0])
    dgr_copy.start()

    def combine(k):
        for p in range(1, nz):
            got(ret.at[k, pl.ds(p * group, group)], ("back", k, p), zdev(p))
        if k == 0:
            coarse = selg[...].astype(BF16)
            fine = (selg[...] - coarse.astype(F32)).astype(BF16)
            summed = tn(coarse, ret[k]) + tn(fine, ret[k])
        else:
            summed = tn(sel[...], ret[k])
        ys[k] = summed.astype(BF16)
        for d in y_order:
            put(
                ys.at[k, pl.ds(d * PAD, PAD)],
                yr.at[k, NY - d],
                ("ys", k, d),
                ("ys", k, NY - d),
                ydev(d),
            )

    def finish(k, out):
        total = ys[k, 0:PAD, :].astype(F32)
        for d in range(1, NY):
            got(yr.at[k, d], ("ys", k, d), ydev(d))
            total = total + yr[k, d].astype(F32)
        out[...] = total[0:token_count, :].astype(BF16)

    combine(0)
    reduce_end(1)
    finish(0, mix_o)
    combine(1)
    finish(1, ing_o)

    dgr_copy.wait()
    for copy in sends:
        copy.wait_send()
    assert len(ssems.index) <= send_sem.shape[0] and len(rsems.index) <= recv_sem.shape[0]


def on_device(hidden_in, expert_ids, gate_weights, out_grad, gate_weight, up_weight, down_weight):
    token_count, per_token = expert_ids.shape
    nz = lax.axis_size("expert") // NY
    width = hidden_in.shape[1]
    hidden = gate_weight.shape[2]
    slots = NX * NC
    rows = nz * NY * CAP
    lanes = NY * PAD
    chunks = 4 if nz % 4 == 0 else 2
    copies = 2 * (NY - 1) * 3 + 4 * (nz - 1) + 2 * 7 * chunks + 64
    vmem = pl.BlockSpec(memory_space=pltpu.VMEM)
    hbm = pl.BlockSpec(memory_space=pl.ANY)
    mixed, input_grad, down_grad = pl.pallas_call(
        functools.partial(kernel, nz, chunks, (token_count, width, hidden)),
        out_shape=(
            jax.ShapeDtypeStruct((token_count, width), BF16),
            jax.ShapeDtypeStruct((token_count, width), BF16),
            jax.ShapeDtypeStruct((hidden, slots * width), BF16),
        ),
        in_specs=[vmem] * 4 + [hbm] * 3,
        out_specs=(vmem, vmem, hbm),
        scratch_shapes=[
            pltpu.VMEM((2, lanes, width), BF16),
            pltpu.VMEM((NY, per_token, lanes), F32),
            pltpu.VMEM((2, rows, width), BF16),
            pltpu.VMEM((2, slots, rows, width), BF16),
            pltpu.VMEM((slots, width, 2 * hidden), BF16),
            pltpu.VMEM((slots, hidden, width), BF16),
            pltpu.VMEM((16, lanes), F32),
            pltpu.VMEM((16, lanes), F32),
            pltpu.VMEM((16, lanes), F32),
            pltpu.VMEM((rows, lanes), BF16),
            pltpu.VMEM((rows, lanes), F32),
            pltpu.VMEM((rows, 2 * hidden), F32),
            pltpu.VMEM((rows, hidden), F32),
            pltpu.VMEM((rows, hidden), BF16),
            pltpu.VMEM((rows, 2 * hidden), BF16),
            pltpu.VMEM((hidden, slots * width), BF16),
            pltpu.VMEM((2, NX, rows, width), BF16),
            pltpu.VMEM((2, NX, rows, width), BF16),
            pltpu.VMEM((2, NX, rows, width), BF16),
            pltpu.VMEM((2, 2, rows // 2, width), BF16),
            pltpu.VMEM((2, 2, rows, width), BF16),
            pltpu.VMEM((2, rows, width), BF16),
            pltpu.VMEM((2, rows, width), BF16),
            pltpu.VMEM((2, lanes, width), BF16),
            pltpu.VMEM((2, NY, PAD, width), BF16),
            pltpu.SemaphoreType.DMA((copies,)),
            pltpu.SemaphoreType.DMA((copies,)),
            pltpu.SemaphoreType.DMA((3 * slots,)),
        ],
        compiler_params=pltpu.CompilerParams(
            collective_id=0, has_side_effects=True, vmem_limit_bytes=48 << 20
        ),
    )(hidden_in, expert_ids, gate_weights, out_grad, gate_weight[0], up_weight[0], down_weight[0])
    return mixed, input_grad, down_grad[None]


def solution(mesh):
    return jax.shard_map(
        on_device,
        mesh=mesh,
        in_specs=(
            P("expert", "etp"),
            P("expert", None),
            P("expert", None),
            P("expert", "etp"),
            P("expert", None, "etp"),
            P("expert", None, "etp"),
            P("expert", "etp", None),
        ),
        out_specs=(P("expert", "etp"), P("expert", "etp"), P("expert", "etp", None)),
        check_vma=False,
    )
```

time: 204 us -> 108 us (0.53)
  Pallas kernels: 0 us -> 98.1 us
  blocking collectives: 85.2 us -> 0 us
  waiting for transfers between devices: 52.2 us -> 0 us
  starting transfers between devices: 16.4 us -> 0 us
  between operations: 14.3 us -> 0.66 us
  local copies, waits for them, and re-layouts: 17.4 us -> 8.1 us
  other arithmetic: 8.4 us -> 0 us
  matrix products: 7.45 us -> 0 us
    pallas_call x0 -> x1, Pallas kernels: none -> 98.1 us  [on_device(): pl.pallas_call(functools.partial(kernel, nz, chunks, (token_count, width,...]
    all_to_all x2 -> x0, blocking collectives: 85.2 us -> none  [the longest x1 44 us: sent_together(): lax.all_to_all(both, axis, split_axis=split_dim, concat_axis=concat_dim,...]
    all_gather x1 -> x0, waiting for transfers between devices: 32.5 us -> none  [side_by_side(): whole = lax.all_gather(both, axis, axis=dim, tiled=True)]
    all_to_all x1 -> x0, waiting for transfers between devices: 19.7 us -> none  [sent_together(): lax.all_to_all(both, axis, split_axis=split_dim, concat_axis=concat_dim,...]
    all_to_all x1 -> x0, starting transfers between devices: 16.4 us -> none  [sent_together(): lax.all_to_all(both, axis, split_axis=split_dim, concat_axis=concat_dim,...]
    dot_general x9 -> x0, matrix products: 7.45 us -> none  [the longest x3 3.1 us: contract_last(): lax.dot_general(left, right, (((1,), (1,)), ((), ())), preferred_element_...]
    reshape x9 -> x0, local copies, waits for them, and re-layouts: 6.9 us -> none  [the longest x1 3.66 us: on_device(): rows_in = rows_in.reshape(experts * capacity, width)]
    split x4 -> x0, local copies, waits for them, and re-layouts: 6.31 us -> none  [the longest x1 5.73 us: side_by_side(): jnp.split(whole, [sum(widths[:k]) for k in range(1, len(widths))], axis=a...]
  transfers between devices with their start and end apart: 2 -> 0, of which waited for: 2 -> 0; matrix products, arithmetic and copies ran while one was open for 1% -> 0% of each run, Pallas kernels for 0% -> 0%
where the time goes in v1:
time: 108 us; the launch traced here: 107 us
  Pallas kernels  98.1 us (91%)
  local copies, waits for them, and re-layouts  8.1 us (8%)
    pallas_call x1, Pallas kernels, on_device(): pl.pallas_call(functools.partial(kernel, nz, chunks, (token_count, width,...  98.1 us
    unnamed x17, local copies, waits for them, and re-layouts  8.1 us

profile of v1, /device:TPU:1, one launch (start us, length us, event | category | flops | bytes accessed | tf_op | source)
XLA Modules:
  0.0 106.9 jit_solution(9067304553723879773)
XLA Ops:
  0.6 0.0 copy-start.5
  0.6 0.0 copy-start.3
  0.6 0.7 copy-done.5
  1.3 0.1 copy.10.refs_1_
  1.4 0.8 copy.11.refs_2_
  2.2 0.0 copy-done.3
  2.2 0.0 copy-start
  2.2 1.2 %copy-done = bf16[1,4096,128]{2,1,0:T(8,128)(2,1)S(1)} copy-done((bf16[1,4096,128]{2,1,0:T(8,128)(2,1)S(1)}, bf16[1,4096,128]{2,1,0:T(8,128)(2,1)}, u32[]{:S(2)}) %copy-start) | copy-done | bytes 1048600
  3.4 0.0 copy-start.1
  3.4 1.2 %copy-done.1 = bf16[1,4096,128]{2,1,0:T(8,128)(2,1)S(1)} copy-done((bf16[1,4096,128]{2,1,0:T(8,128)(2,1)S(1)}, bf16[1,4096,128]{2,1,0:T(8,128)(2,1)}, u32[]{:S(2)}) %copy-start.1) | copy-done | bytes 1048600
  4.6 0.0 copy-start.2
  4.6 1.2 %copy-done.2 = bf16[1,128,4096]{2,1,0:T(8,128)(2,1)S(1)} copy-done((bf16[1,128,4096]{2,1,0:T(8,128)(2,1)S(1)}, bf16[1,128,4096]{2,1,0:T(8,128)(2,1)}, u32[]{:S(2)}) %copy-start.2) | copy-done | bytes 1048600
  5.8 0.0 copy-start.4
  5.9 0.7 copy-done.4
  6.6 98.1 %shard_map.94 = (bf16[12,512]{1,0:T(8,128)(2,1)S(1)}, bf16[12,512]{1,0:T(8,128)(2,1)S(1)}, bf16[128,4096]{1,0:T(8,128)(2,1)S(1)}) custom-call(bf16[12,512]{1,0:T(8,128)(2,1)S(1)} %copy-done.3, s32[12,8]{1,0:T(8,128)S(1)} %copy.10.refs_1_, f32[12,8]{1,0:T(8,128)S(1)} %copy.11.refs_2_, bf16[12,512]{1,0:T(8,128)(2,1)S(1)} %copy-done.4, ...), custom_call_target="tpu_custom_call" | custom-call | tf_op jit(solution)/shard_map/pallas_call | solution.py:395
  104.7 0.6 copy.15
  105.3 0.6 copy.16
  105.9 1.0 copy.17
Async XLA Ops:
  0.6 0.7 copy-start.5
  0.6 1.5 %copy-start.3 = (bf16[12,512]{1,0:T(8,128)(2,1)S(1)}, bf16[12,512]{1,0:T(8,128)(2,1)}, u32[]{:S(2)}) copy-start(bf16[12,512]{1,0:T(8,128)(2,1)} %refs_0_.1) | copy-start | bytes 36868
  2.2 1.2 %copy-start = (bf16[1,4096,128]{2,1,0:T(8,128)(2,1)S(1)}, bf16[1,4096,128]{2,1,0:T(8,128)(2,1)}, u32[]{:S(2)}) copy-start(bf16[1,4096,128]{2,1,0:T(8,128)(2,1)} %param.11) | copy-start | bytes 3145732
  3.4 1.2 %copy-start.1 = (bf16[1,4096,128]{2,1,0:T(8,128)(2,1)S(1)}, bf16[1,4096,128]{2,1,0:T(8,128)(2,1)}, u32[]{:S(2)}) copy-start(bf16[1,4096,128]{2,1,0:T(8,128)(2,1)} %param.12) | copy-start | bytes 3145732
  4.6 1.2 %copy-start.2 = (bf16[1,128,4096]{2,1,0:T(8,128)(2,1)S(1)}, bf16[1,128,4096]{2,1,0:T(8,128)(2,1)}, u32[]{:S(2)}) copy-start(bf16[1,128,4096]{2,1,0:T(8,128)(2,1)} %param.13) | copy-start | bytes 3145732
  5.8 0.7 copy-start.4

commit v2 on v1

--- a/solution.py
+++ b/solution.py
@@ -24,18 +24,18 @@
     return out
 
 
-def nn(a, b):
-    return lax.dot_general(a, b, (((1,), (0,)), ((), ())), preferred_element_type=F32)
+def nn(a, b, precision=None):
+    return lax.dot_general(
+        a, b, (((1,), (0,)), ((), ())), precision=precision, preferred_element_type=F32
+    )
 
 
 def nt(a, b):
     return lax.dot_general(a, b, (((1,), (1,)), ((), ())), preferred_element_type=F32)
 
 
-def tn(a, b, precision=None):
-    return lax.dot_general(
-        a, b, (((0,), (0,)), ((), ())), precision=precision, preferred_element_type=F32
-    )
+def tn(a, b):
+    return lax.dot_general(a, b, (((0,), (0,)), ((), ())), preferred_element_type=F32)
 
 
 class Sems:
@@ -47,10 +47,10 @@
 
 
 def kernel(nz, chunks, sizes, *refs):
-    (hid, ids, gat, og, wg_hbm, wu_hbm, wd_hbm) = refs[:7]
+    (hid_hbm, ids_hbm, gat_hbm, og_hbm, wg_hbm, wu_hbm, wd_hbm) = refs[:7]
     (mix_o, ing_o, dgr_o) = refs[7:10]
-    (tok, rt, zs, g, wgu, dn, asc, csc, gsc, sel, selg, pre, agr, hact, gug, dgr) = refs[10:26]
-    (pps, ppr, chip, d2r, nbr, fin, ret, ys, yr, send_sem, recv_sem, loc_sem) = refs[26:]
+    (hid, ids, gat, og, tok, rt, zs, g, wgu, dn, asc, csc, gsc, sel, selg, pre, agr, hact, gug, dgr) = refs[10:30]
+    (pps, ppr, chip, d2r, nbr, fin, ret, ys, yr, send_sem, recv_sem, loc_sem) = refs[30:]
     token_count, width, hidden = sizes
     x_t = lax.axis_index("etp")
     x_e = lax.axis_index("expert")
@@ -105,7 +105,11 @@
             device_id_type=MESH,
         ).wait_recv()
 
-    loads = []
+    small, loads = [], []
+    for i, (src, dst) in enumerate(((ids_hbm, ids), (gat_hbm, gat), (hid_hbm, hid), (og_hbm, og))):
+        copy = pltpu.make_async_copy(src, dst, loc_sem.at[3 * slots + i])
+        copy.start()
+        small.append(copy)
     for t in range(slots):
         cols = pl.ds(t * width, width)
         for src, dst in (
@@ -123,6 +127,8 @@
     for dev in peers:
         pl.semaphore_signal(barrier, inc=1, device_id=dev, device_id_type=MESH)
 
+    for copy in small:
+        copy.wait()
     for k, src in ((0, hid), (1, og)):
         tok[k, 0:PAD, :] = jnp.zeros((PAD, width), BF16)
         tok[k, 0:token_count, :] = src[...]
@@ -130,7 +136,7 @@
     row_t = lax.broadcasted_iota(jnp.int32, (token_count, lanes), 0)
     here = lax.rem(lane_t, PAD) == row_t
     exact = lax.Precision.HIGHEST
-    rt[0] = tn(ids[...].astype(F32), jnp.where(here & (lane_t < half), 1.0, 0.0), exact) + tn(
+    rt[0] = nn(ids[...].astype(F32), jnp.where(here & (lane_t < half), 1.0, 0.0), exact) + nn(
         gat[...], jnp.where(here & (lane_t >= half), 1.0, 0.0), exact
     )
 
@@ -180,7 +186,7 @@
         sel[p * group : (p + 1) * group, :] = pick.astype(BF16)
         selg[p * group : (p + 1) * group, :] = pick * gsc[p : p + 1, :]
 
-    z_order = sorted(range(1, nz), key=lambda p: -p)
+    z_order = range(1, nz)
     for k in (0, 1):
         for d in range(1, NY):
             got(tok.at[k, pl.ds(d * PAD, PAD)], ("tok", k, d), ydev(d))
@@ -230,78 +236,111 @@
     steps = [(k, j) for k in (0, 1) for j in range(chunks)]
 
     def step(s):
-        if 0 <= s < len(steps):
-            pass_own(*steps[s])
-        if 0 <= s - 1 < len(steps):
-            pass_near(*steps[s - 1])
-        if 0 <= s - 2 < len(steps):
-            pass_far(*steps[s - 2])
+        for wait, pass_on in ((s, pass_own), (s - 4, pass_far), (s - 2, pass_near)):
+            if 0 <= wait < len(steps):
+                pass_on(*steps[wait])
 
     def wait_other(k):
         for dx in (0, 3, 1, 2):
             for j in range(chunks):
                 got(piece(k, j, tab(dx, 1)), ("g", k, j, "o%d" % dx), partner)
 
-    for s in range(chunks + 2):
+    for s in range(chunks):
         step(s)
     pre[...] = nn(g[0, tab(0)], wgu[tab(0)])
-    for dx in (3, 1, 2):
+    for s in range(chunks, chunks + 2):
+        step(s)
+    for dx in (3, 1):
         pre[...] += nn(g[0, tab(dx)], wgu[tab(dx)])
+    for s in range(chunks + 2, 2 * chunks):
+        step(s)
+    pre[...] += nn(g[0, tab(2)], wgu[tab(2)])
     wait_other(0)
     for dx in (0, 3, 1, 2):
         pre[...] += nn(g[0, tab(dx, 1)], wgu[tab(dx, 1)])
     gate_pre, up_pre = pre[:, 0:hidden], pre[:, hidden : 2 * hidden]
     hact[...] = (gate_pre * jax.nn.sigmoid(gate_pre) * up_pre).astype(BF16)
 
-    def part(k, t):
-        return nn(hact[...], dn[t]) if k == 0 else nt(gug[...], wgu[t])
-
-    order = (2, 1, 3, 0)
-
-    def reduce_pair_send(k):
-        for dx in order:
-            pps[k, dx] = part(k, tab(dx, 1)).astype(BF16)
-            put(pps.at[k, dx], ppr.at[k, dx], ("pp", k, dx), ("pp", k, dx), partner)
-
-    first, second = pl.ds(0, rows // 2), pl.ds(rows // 2, rows // 2)
-
-    def reduce_pair(k, dx):
-        mine = part(k, tab(dx))
-        got(ppr.at[k, dx], ("pp", k, dx), partner)
-        chip[k, dx] = (mine + ppr[k, dx].astype(F32)).astype(BF16)
-
-    def reduce_start(k):
-        reduce_pair(k, 2)
-        put(chip.at[k, 2, first], d2r.at[k, 0], ("d2", k, 0), ("d2", k, 0), xdev(1))
-        put(chip.at[k, 2, second], d2r.at[k, 1], ("d2", k, 1), ("d2", k, 1), xdev(3))
-        reduce_pair(k, 1)
-        put(chip.at[k, 1, second], nbr.at[k, 0, second], ("n", k, 0, 1), ("n", k, 0, 1), xdev(1))
-        reduce_pair(k, 3)
-        put(chip.at[k, 3, first], nbr.at[k, 1, first], ("n", k, 1, 0), ("n", k, 1, 0), xdev(3))
-        reduce_pair(k, 0)
-
-    def reduce_relay(k):
-        for i, (dx, part_rows) in enumerate(((1, first), (3, second))):
-            got(d2r.at[k, i], ("d2", k, i), xdev(4 - dx))
-            chip[k, dx, part_rows] = (
-                chip[k, dx, part_rows].astype(F32) + d2r[k, i].astype(F32)
+    def span(h):
+        return pl.ds(h * (rows // 2), rows // 2)
+
+    left, right = pl.ds(0, width // 2), pl.ds(width // 2, width // 2)
+
+    def part(k, h, t):
+        if k == 0:
+            return nn(hact[span(h), :], dn[t])
+        return nt(gug[span(h), :], wgu[t])
+
+    def pair_send(k, h, dx):
+        pps[k, dx, span(h), :] = part(k, h, tab(dx, 1)).astype(BF16)
+        put(
+            pps.at[k, dx, span(h)],
+            ppr.at[k, dx, span(h)],
+            ("pp", k, h, dx),
+            ("pp", k, h, dx),
+            partner,
+        )
+
+    def pair_sum(k, h, dx):
+        mine = part(k, h, tab(dx))
+        got(ppr.at[k, dx, span(h)], ("pp", k, h, dx), partner)
+        chip[k, dx, span(h), :] = (mine + ppr[k, dx, span(h), :].astype(F32)).astype(BF16)
+        if dx == 2:
+            for i, (cols, to) in enumerate(((left, 1), (right, 3))):
+                put(
+                    chip.at[k, 2, span(h), cols],
+                    d2r.at[k, i, span(h)],
+                    ("d2", k, h, i),
+                    ("d2", k, h, i),
+                    xdev(to),
+                )
+        elif dx:
+            i, cols = (0, right) if dx == 1 else (1, left)
+            put(
+                chip.at[k, dx, span(h), cols],
+                nbr.at[k, i, span(h), cols],
+                ("n", k, h, i, "direct"),
+                ("n", k, h, i, "direct"),
+                xdev(dx),
+            )
+
+    def reduce_start(k, h):
+        pair_send(k, h, 2)
+        pair_send(k, h, 1)
+        pair_sum(k, h, 2)
+        pair_send(k, h, 3)
+        pair_sum(k, h, 1)
+        pair_send(k, h, 0)
+        pair_sum(k, h, 3)
+        pair_sum(k, h, 0)
+
+    def reduce_relay(k, h):
+        for i, (dx, cols) in enumerate(((1, left), (3, right))):
+            got(d2r.at[k, i, span(h)], ("d2", k, h, i), xdev(4 - dx))
+            chip[k, dx, span(h), cols] = (
+                chip[k, dx, span(h), cols].astype(F32) + d2r[k, i, span(h), :].astype(F32)
             ).astype(BF16)
             put(
-                chip.at[k, dx, part_rows],
-                nbr.at[k, i, part_rows],
-                ("n", k, i, i),
-                ("n", k, i, i),
+                chip.at[k, dx, span(h), cols],
+                nbr.at[k, i, span(h), cols],
+                ("n", k, h, i, "relay"),
+                ("n", k, h, i, "relay"),
                 xdev(dx),
             )
 
-    def reduce_end(k):
-        for i in (0, 1):
-            for h, part_rows in enumerate((first, second)):
-                got(nbr.at[k, i, part_rows], ("n", k, i, h), xdev(3 if i == 0 else 1))
-        fin[k] = (
-            chip[k, 0].astype(F32) + nbr[k, 0].astype(F32) + nbr[k, 1].astype(F32)
+    def reduce_end(k, h):
+        for i, (direct, relayed) in enumerate(((right, left), (left, right))):
+            came = xdev(3 if i == 0 else 1)
+            got(nbr.at[k, i, span(h), direct], ("n", k, h, i, "direct"), came)
+            got(nbr.at[k, i, span(h), relayed], ("n", k, h, i, "relay"), came)
+        fin[k, span(h), :] = (
+            chip[k, 0, span(h), :].astype(F32)
+            + nbr[k, 0, span(h), :].astype(F32)
+            + nbr[k, 1, span(h), :].astype(F32)
         ).astype(BF16)
-        for p in z_order:
+        for p in range(h * (nz // 2), (h + 1) * (nz // 2)):
+            if p == 0:
+                continue
             q = neg(p)
             put(
                 fin.at[k, pl.ds(p * group, group)],
@@ -310,18 +349,21 @@
                 ("back", k, q),
                 zdev(p),
             )
-        ret[k, 0:group, :] = fin[k, 0:group, :]
-
-    reduce_pair_send(0)
-    step(chunks + 2)
-    step(chunks + 3)
-    reduce_start(0)
-    for s in range(chunks + 4, 2 * chunks + 2):
-        step(s)
+        if h == 0:
+            ret[k, 0:group, :] = fin[k, 0:group, :]
+
+    reduce_start(0, 1)
+    step(2 * chunks)
+    step(2 * chunks + 1)
+    reduce_start(0, 0)
+    step(2 * chunks + 2)
+    step(2 * chunks + 3)
+    reduce_relay(0, 1)
 
     agr[...] = nt(g[1, tab(0)], dn[tab(0)])
     for dx in (3, 1, 2):
         agr[...] += nt(g[1, tab(dx)], dn[tab(dx)])
+    reduce_relay(0, 0)
     wait_other(1)
     for dx in (0, 3, 1, 2):
         agr[...] += nt(g[1, tab(dx, 1)], dn[tab(dx, 1)])
@@ -331,14 +373,20 @@
     gug[:, 0:hidden] = (act_grad * up_pre * sig * (1.0 + gate_pre * (1.0 - sig))).astype(BF16)
     gug[:, hidden : 2 * hidden] = (act_grad * (gate_pre * sig)).astype(BF16)
 
-    reduce_pair_send(1)
-    reduce_relay(0)
-    reduce_start(1)
-    reduce_end(0)
-    reduce_relay(1)
-
-    for t in range(slots):
+    reduce_start(1, 1)
+    reduce_end(0, 1)
+    reduce_start(1, 0)
+    reduce_end(0, 0)
+    reduce_relay(1, 1)
+
+    def weight_grad(t):
         dgr[:, t * width : (t + 1) * width] = tn(hact[...], g[1, t]).astype(BF16)
+
+    for t in range(slots // 2):
+        weight_grad(t)
+    reduce_relay(1, 0)
+    for t in range(slots // 2, slots):
+        weight_grad(t)
     dgr_copy = pltpu.make_async_copy(dgr, dgr_o, loc_sem.at[0])
     dgr_copy.start()
 
@@ -368,10 +416,11 @@
             total = total + yr[k, d].astype(F32)
         out[...] = total[0:token_count, :].astype(BF16)
 
+    reduce_end(1, 1)
     combine(0)
-    reduce_end(1)
+    reduce_end(1, 0)
+    combine(1)
     finish(0, mix_o)
-    combine(1)
     finish(1, ing_o)
 
     dgr_copy.wait()
@@ -389,9 +438,9 @@
     rows = nz * NY * CAP
     lanes = NY * PAD
     chunks = 4 if nz % 4 == 0 else 2
-    copies = 2 * (NY - 1) * 3 + 4 * (nz - 1) + 2 * 7 * chunks + 64
+    copies = 2 * (NY - 1) * 3 + 4 * (nz - 1) + 2 * 7 * chunks + 96
     vmem = pl.BlockSpec(memory_space=pltpu.VMEM)
-    hbm = pl.BlockSpec(memory_space=pl.ANY)
+    hbm = pl.BlockSpec(memory_space=pltpu.HBM)
     mixed, input_grad, down_grad = pl.pallas_call(
         functools.partial(kernel, nz, chunks, (token_count, width, hidden)),
         out_shape=(
@@ -399,9 +448,13 @@
             jax.ShapeDtypeStruct((token_count, width), BF16),
             jax.ShapeDtypeStruct((hidden, slots * width), BF16),
         ),
-        in_specs=[vmem] * 4 + [hbm] * 3,
+        in_specs=[hbm] * 7,
         out_specs=(vmem, vmem, hbm),
         scratch_shapes=[
+            pltpu.VMEM((token_count, width), BF16),
+            pltpu.VMEM((per_token, token_count), jnp.int32),
+            pltpu.VMEM((per_token, token_count), F32),
+            pltpu.VMEM((token_count, width), BF16),
             pltpu.VMEM((2, lanes, width), BF16),
             pltpu.VMEM((NY, per_token, lanes), F32),
             pltpu.VMEM((2, rows, width), BF16),
@@ -421,7 +474,7 @@
             pltpu.VMEM((2, NX, rows, width), BF16),
             pltpu.VMEM((2, NX, rows, width), BF16),
             pltpu.VMEM((2, NX, rows, width), BF16),
-            pltpu.VMEM((2, 2, rows // 2, width), BF16),
+            pltpu.VMEM((2, 2, rows, width // 2), BF16),
             pltpu.VMEM((2, 2, rows, width), BF16),
             pltpu.VMEM((2, rows, width), BF16),
             pltpu.VMEM((2, rows, width), BF16),
@@ -429,12 +482,25 @@
             pltpu.VMEM((2, NY, PAD, width), BF16),
             pltpu.SemaphoreType.DMA((copies,)),
             pltpu.SemaphoreType.DMA((copies,)),
-            pltpu.SemaphoreType.DMA((3 * slots,)),
+            pltpu.SemaphoreType.DMA((3 * slots + 4,)),
         ],
         compiler_params=pltpu.CompilerParams(
             collective_id=0, has_side_effects=True, vmem_limit_bytes=48 << 20
         ),
-    )(hidden_in, expert_ids, gate_weights, out_grad, gate_weight[0], up_weight[0], down_weight[0])
+    )(
+        *(
+            pltpu.with_memory_space_constraint(a, pltpu.HBM)
+            for a in (
+                hidden_in,
+                expert_ids.T,
+                gate_weights.T,
+                out_grad,
+                gate_weight[0],
+                up_weight[0],
+                down_weight[0],
+            )
+        )
+    )
     return mixed, input_grad, down_grad[None]
 
 

time: 108 us -> 88.4 us (0.82)
  Pallas kernels: 98.1 us -> 85.4 us
  local copies, waits for them, and re-layouts: 8.1 us -> 2.18 us
    pallas_call x1, Pallas kernels: 98.1 us -> 85.4 us  [on_device(): pl.pallas_call(functools.partial(kernel, nz, chunks, (token_count, width,...]
    unnamed x17 -> x3, local copies, waits for them, and re-layouts: 8.1 us -> 2.18 us
where the time goes in v2:
time: 88.4 us; the launch traced here: 88.3 us
  Pallas kernels  85.4 us (97%)
  local copies, waits for them, and re-layouts  2.18 us (2%)
    pallas_call x1, Pallas kernels, on_device(): pl.pallas_call(functools.partial(kernel, nz, chunks, (token_count, width,...  85.4 us
    unnamed x3, local copies, waits for them, and re-layouts  2.18 us

profile of v2, /device:TPU:1, one launch (start us, length us, event | category | flops | bytes accessed | tf_op | source)
XLA Modules:
  0.0 88.3 jit_solution(14653069918595722795)
XLA Ops:
  0.6 85.4 %shard_map.94 = (bf16[12,512]{1,0:T(8,128)(2,1)S(1)}, bf16[12,512]{1,0:T(8,128)(2,1)S(1)}, bf16[128,4096]{1,0:T(8,128)(2,1)S(1)}) custom-call(bf16[12,512]{1,0:T(8,128)(2,1)} %refs_0_.1, s32[8,12]{1,0:T(8,128)} %bitcast.10, f32[8,12]{1,0:T(8,128)} %bitcast.11, bf16[12,512]{1,0:T(8,128)(2,1)} %refs_3_.1, bf16[4096,128]{1,0:T(8,128)(2,1)} %bitcast.7, ...), custom_call_target="tpu_custom_call" | custom-call | tf_op jit(solution)/shard_map/pallas_call | solution.py:444
  86.1 0.6 copy.13
  86.7 0.6 copy.14
  87.3 1.0 %copy.15 = bf16[1,128,4096]{2,1,0:T(8,128)(2,1)} copy(bf16[1,128,4096]{2,1,0:T(8,128)(2,1)S(1)} %bitcast.6) | data formatting | bytes 2097152

commit v3 on v2

--- a/solution.py
+++ b/solution.py
@@ -50,7 +50,7 @@
     (hid_hbm, ids_hbm, gat_hbm, og_hbm, wg_hbm, wu_hbm, wd_hbm) = refs[:7]
     (mix_o, ing_o, dgr_o) = refs[7:10]
     (hid, ids, gat, og, tok, rt, zs, g, wgu, dn, asc, csc, gsc, sel, selg, pre, agr, hact, gug, dgr) = refs[10:30]
-    (pps, ppr, chip, d2r, nbr, fin, ret, ys, yr, send_sem, recv_sem, loc_sem) = refs[30:]
+    (pps, ppr, chip, nbr, fin, ret, ys, yr, send_sem, recv_sem, loc_sem) = refs[30:]
     token_count, width, hidden = sizes
     x_t = lax.axis_index("etp")
     x_e = lax.axis_index("expert")
@@ -122,7 +122,7 @@
             loads.append(copy)
 
     peers = [zdev(p) for p in range(1, nz)] + [ydev(d) for d in range(1, NY)]
-    peers += [xdev(1), xdev(3), partner]
+    peers += [xdev(1), xdev(2), xdev(3), partner]
     barrier = pltpu.get_barrier_semaphore()
     for dev in peers:
         pl.semaphore_signal(barrier, inc=1, device_id=dev, device_id_type=MESH)
@@ -216,27 +216,26 @@
             if p:
                 got(g.at[k, x_t, pl.ds(p * group, group)], ("z", k, p), zdev(p))
         own = piece(k, j, x_t)
-        put(own, own, ("g", k, j, "own+"), ("g", k, j, 3), xdev(1))
-        put(own, own, ("g", k, j, "own-"), ("g", k, j, 1), xdev(3))
-        put(own, own, ("g", k, j, "own|"), ("g", k, j, "o0"), partner)
+        for dx in (1, 3, 2):
+            put(own, own, ("g", k, j, NX - dx), ("g", k, j, NX - dx), xdev(dx))
+        put(own, own, ("g", k, j, "o0"), ("g", k, j, "o0"), partner)
+
+    def hand_over(k, j, dx):
+        ref = piece(k, j, tab(dx))
+        got(ref, ("g", k, j, dx), xdev(dx))
+        put(ref, ref, ("g", k, j, "o%d" % dx), ("g", k, j, "o%d" % dx), partner)
 
     def pass_near(k, j):
         for dx in (3, 1):
-            ref = piece(k, j, tab(dx))
-            got(ref, ("g", k, j, dx), xdev(dx))
-            if (j % 2 == 0) == (dx == 3):
-                put(ref, ref, ("g", k, j, "far"), ("g", k, j, 2), xdev(4 - dx))
-            put(ref, ref, ("g", k, j, "near|", dx), ("g", k, j, "o%d" % dx), partner)
+            hand_over(k, j, dx)
 
     def pass_far(k, j):
-        ref = piece(k, j, tab(2))
-        got(ref, ("g", k, j, 2), xdev(3))
-        put(ref, ref, ("g", k, j, "far|"), ("g", k, j, "o2"), partner)
+        hand_over(k, j, 2)
 
     steps = [(k, j) for k in (0, 1) for j in range(chunks)]
 
     def step(s):
-        for wait, pass_on in ((s, pass_own), (s - 4, pass_far), (s - 2, pass_near)):
+        for wait, pass_on in ((s, pass_own), (s - 3, pass_far), (s - 2, pass_near)):
             if 0 <= wait < len(steps):
                 pass_on(*steps[wait])
 
@@ -264,8 +263,6 @@
     def span(h):
         return pl.ds(h * (rows // 2), rows // 2)
 
-    left, right = pl.ds(0, width // 2), pl.ds(width // 2, width // 2)
-
     def part(k, h, t):
         if k == 0:
             return nn(hact[span(h), :], dn[t])
@@ -285,22 +282,12 @@
         mine = part(k, h, tab(dx))
         got(ppr.at[k, dx, span(h)], ("pp", k, h, dx), partner)
         chip[k, dx, span(h), :] = (mine + ppr[k, dx, span(h), :].astype(F32)).astype(BF16)
-        if dx == 2:
-            for i, (cols, to) in enumerate(((left, 1), (right, 3))):
-                put(
-                    chip.at[k, 2, span(h), cols],
-                    d2r.at[k, i, span(h)],
-                    ("d2", k, h, i),
-                    ("d2", k, h, i),
-                    xdev(to),
-                )
-        elif dx:
-            i, cols = (0, right) if dx == 1 else (1, left)
+        if dx:
             put(
-                chip.at[k, dx, span(h), cols],
-                nbr.at[k, i, span(h), cols],
-                ("n", k, h, i, "direct"),
-                ("n", k, h, i, "direct"),
+                chip.at[k, dx, span(h)],
+                nbr.at[k, NX - dx, span(h)],
+                ("n", k, h, NX - dx),
+                ("n", k, h, NX - dx),
                 xdev(dx),
             )
 
@@ -314,30 +301,12 @@
         pair_sum(k, h, 3)
         pair_sum(k, h, 0)
 
-    def reduce_relay(k, h):
-        for i, (dx, cols) in enumerate(((1, left), (3, right))):
-            got(d2r.at[k, i, span(h)], ("d2", k, h, i), xdev(4 - dx))
-            chip[k, dx, span(h), cols] = (
-                chip[k, dx, span(h), cols].astype(F32) + d2r[k, i, span(h), :].astype(F32)
-            ).astype(BF16)
-            put(
-                chip.at[k, dx, span(h), cols],
-                nbr.at[k, i, span(h), cols],
-                ("n", k, h, i, "relay"),
-                ("n", k, h, i, "relay"),
-                xdev(dx),
-            )
-
     def reduce_end(k, h):
-        for i, (direct, relayed) in enumerate(((right, left), (left, right))):
-            came = xdev(3 if i == 0 else 1)
-            got(nbr.at[k, i, span(h), direct], ("n", k, h, i, "direct"), came)
-            got(nbr.at[k, i, span(h), relayed], ("n", k, h, i, "relay"), came)
-        fin[k, span(h), :] = (
-            chip[k, 0, span(h), :].astype(F32)
-            + nbr[k, 0, span(h), :].astype(F32)
-            + nbr[k, 1, span(h), :].astype(F32)
-        ).astype(BF16)
+        total = chip[k, 0, span(h), :].astype(F32)
+        for dx in (3, 1, 2):
+            got(nbr.at[k, dx, span(h)], ("n", k, h, dx), xdev(dx))
+            total = total + nbr[k, dx, span(h), :].astype(F32)
+        fin[k, span(h), :] = total.astype(BF16)
         for p in range(h * (nz // 2), (h + 1) * (nz // 2)):
             if p == 0:
                 continue
@@ -352,18 +321,15 @@
         if h == 0:
             ret[k, 0:group, :] = fin[k, 0:group, :]
 
+    step(2 * chunks)
     reduce_start(0, 1)
-    step(2 * chunks)
-    step(2 * chunks + 1)
+    for s in range(2 * chunks + 1, 2 * chunks + 3):
+        step(s)
     reduce_start(0, 0)
-    step(2 * chunks + 2)
-    step(2 * chunks + 3)
-    reduce_relay(0, 1)
 
     agr[...] = nt(g[1, tab(0)], dn[tab(0)])
     for dx in (3, 1, 2):
         agr[...] += nt(g[1, tab(dx)], dn[tab(dx)])
-    reduce_relay(0, 0)
     wait_other(1)
     for dx in (0, 3, 1, 2):
         agr[...] += nt(g[1, tab(dx, 1)], dn[tab(dx, 1)])
@@ -377,15 +343,11 @@
     reduce_end(0, 1)
     reduce_start(1, 0)
     reduce_end(0, 0)
-    reduce_relay(1, 1)
 
     def weight_grad(t):
         dgr[:, t * width : (t + 1) * width] = tn(hact[...], g[1, t]).astype(BF16)
 
-    for t in range(slots // 2):
-        weight_grad(t)
-    reduce_relay(1, 0)
-    for t in range(slots // 2, slots):
+    for t in range(slots):
         weight_grad(t)
     dgr_copy = pltpu.make_async_copy(dgr, dgr_o, loc_sem.at[0])
     dgr_copy.start()
@@ -417,8 +379,8 @@
         out[...] = total[0:token_count, :].astype(BF16)
 
     reduce_end(1, 1)
+    reduce_end(1, 0)
     combine(0)
-    reduce_end(1, 0)
     combine(1)
     finish(0, mix_o)
     finish(1, ing_o)
@@ -474,8 +436,7 @@
             pltpu.VMEM((2, NX, rows, width), BF16),
             pltpu.VMEM((2, NX, rows, width), BF16),
             pltpu.VMEM((2, NX, rows, width), BF16),
-            pltpu.VMEM((2, 2, rows, width // 2), BF16),
-            pltpu.VMEM((2, 2, rows, width), BF16),
+            pltpu.VMEM((2, NX, rows, width), BF16),
             pltpu.VMEM((2, rows, width), BF16),
             pltpu.VMEM((2, rows, width), BF16),
             pltpu.VMEM((2, lanes, width), BF16),

time: 88.4 us -> 85.2 us (0.964)
  Pallas kernels: 85.4 us -> 82.2 us
    pallas_call x1, Pallas kernels: 85.4 us -> 82.2 us  [on_device(): pl.pallas_call(functools.partial(kernel, nz, chunks, (token_count, width,...]
where the time goes in v3:
time: 85.2 us; the launch traced here: 85.1 us
  Pallas kernels  82.2 us (96%)
  local copies, waits for them, and re-layouts  2.18 us (3%)
    pallas_call x1, Pallas kernels, on_device(): pl.pallas_call(functools.partial(kernel, nz, chunks, (token_count, width,...  82.2 us
    unnamed x3, local copies, waits for them, and re-layouts  2.18 us

profile of v3, /device:TPU:1, one launch (start us, length us, event | category | flops | bytes accessed | tf_op | source)
XLA Modules:
  0.0 85.1 jit_solution(3644772676231510852)
XLA Ops:
  0.6 82.2 %shard_map.94 = (bf16[12,512]{1,0:T(8,128)(2,1)S(1)}, bf16[12,512]{1,0:T(8,128)(2,1)S(1)}, bf16[128,4096]{1,0:T(8,128)(2,1)S(1)}) custom-call(bf16[12,512]{1,0:T(8,128)(2,1)} %refs_0_.1, s32[8,12]{1,0:T(8,128)} %bitcast.10, f32[8,12]{1,0:T(8,128)} %bitcast.11, bf16[12,512]{1,0:T(8,128)(2,1)} %refs_3_.1, bf16[4096,128]{1,0:T(8,128)(2,1)} %bitcast.7, ...), custom_call_target="tpu_custom_call" | custom-call | tf_op jit(solution)/shard_map/pallas_call | solution.py:406
  82.9 0.6 copy.13
  83.5 0.6 copy.14
  84.1 1.0 %copy.15 = bf16[1,128,4096]{2,1,0:T(8,128)(2,1)} copy(bf16[1,128,4096]{2,1,0:T(8,128)(2,1)S(1)} %bitcast.6) | data formatting | bytes 2097152
